TPU v7x, 512 devices: a whole 4x8x8 slice. The times are simulated.
512 devices in a mesh: ctx: 64 (over y_hi, x, z), exp: 8 (over y_lo, core).
Axes of the slice: x: 4, y: 8 (y_hi: 2, y_lo: 4; y = y_hi * 4 + y_lo), z: 8, core: 2. Of those that a mesh axis runs over, the one named last changes fastest.
Arguments:
- queries: bfloat16 [4096, 6144], P('ctx', 'exp'), may hold values from -5 to 5
- keys: bfloat16 [4096, 1024], P('ctx', 'exp'), may hold values from -5 to 5
- values: bfloat16 [4096, 1024], P('ctx', 'exp'), may hold values from -16 to 16
- residual: bfloat16 [4096, 6144], P('ctx', 'exp'), may hold values from -25 to 25
- norm_gain: float32 [6144], P('exp'), may hold values from 0.5 to 1.5
- routes: int32 [4096, 1], P('ctx'), may hold values from 0 to 3; in each aligned block of 64 rows (0 to 63, 64 to 127, ...) at most 24 rows name the same one
- route_weight: float32 [4096], P('ctx'), may hold values from 0.25 to 1
- w_gate: bfloat16 [65536, 6144], P('ctx', 'exp'), may hold values from -0.078125 to 0.078125
- w_up: bfloat16 [65536, 6144], P('ctx', 'exp'), may hold values from -0.078125 to 0.078125
- w_down: bfloat16 [65536, 6144], P('ctx', 'exp'), may hold values from -0.046875 to 0.046875
Outputs:
- moe_out: bfloat16 [4096, 6144], P('ctx', 'exp')
Inputs may be any that keep to these rules, and one draw needn't show every extreme that they name: `routes`: within the 64 rows of one device, at most 24 tokens have the same route.
All inputs are finite; a program needn't handle non-finite values.
Results may differ from a plain program's by a relative error of at most 0.029.
Values may be sent and summed in bfloat16 or wider, within the bound.
No kernel may reach another device: no remote copies, remote signals or barrier semaphores. Data moves between devices by JAX's collectives and lax.ppermute only.
A program may use at most 64 MiB of HBM per device.

v0:
```python
import math
import jax
import jax.numpy as jnp
from jax import lax
from jax.sharding import PartitionSpec as P

D = 6144
HD = 128
EXPERTS = 4
CAP = 24


def body(queries, keys, values, residual, norm_gain, routes, route_weight, w_gate, w_up, w_down):
    tok_rows = queries.shape[0]
    heads_kv = keys.shape[1] // HD
    heads_query = queries.shape[1] // HD
    group_size = heads_query // heads_kv
    first_pos = lax.axis_index("ctx") * tok_rows
    last_pos = first_pos + tok_rows - 1
    score_scale = 1.0 / math.sqrt(HD)
    query_block = (
        queries.reshape(tok_rows, heads_kv, group_size, HD)
        .transpose(1, 2, 0, 3)
        .reshape(heads_kv, group_size * tok_rows, HD)
    )
    query_pos = first_pos + jnp.tile(jnp.arange(tok_rows, dtype=jnp.int32), group_size)
    initial = (
        jnp.full((heads_kv, group_size * tok_rows), -1e30, jnp.float32),
        jnp.zeros((heads_kv, group_size * tok_rows), jnp.float32),
        jnp.zeros((heads_kv, group_size * tok_rows, HD), jnp.float32),
    )
    key_shard = lax.all_gather(keys, "ctx", axis=0, tiled=True)
    value_shard = lax.all_gather(values, "ctx", axis=0, tiled=True)
    key_count = key_shard.shape[0]

    def compute(status):
        running_max, running_sum, running_acc = status
        key_block = key_shard.reshape(key_count, heads_kv, HD).transpose(1, 0, 2)
        value_block = value_shard.reshape(key_count, heads_kv, HD).transpose(1, 0, 2)
        scores = (
            jnp.einsum("gqd,gkd->gqk", query_block, key_block, preferred_element_type=jnp.float32)
            * score_scale
        )
        key_pos = jnp.arange(key_count, dtype=jnp.int32)
        allowed = (key_pos[None, :] <= query_pos[:, None])[None, :, :]
        masked = jnp.where(allowed, scores, -1e30)
        fresh_max = jnp.maximum(running_max, jnp.max(masked, axis=2))
        weights = jnp.where(allowed, jnp.exp(masked - fresh_max[:, :, None]), 0.0)
        new_sum = jnp.sum(weights, axis=2)
        products = jnp.einsum(
            "gqk,gkd->gqd",
            weights.astype(jnp.bfloat16),
            value_block,
            preferred_element_type=jnp.float32,
        )
        return (fresh_max, new_sum, products)

    def unchanged(status):
        return status

    final_max, final_sum, final_acc = lax.cond(
        jnp.int32(0) <= last_pos, compute, unchanged, initial
    )
    attn_heads = final_acc / final_sum[:, :, None]
    attn = (
        attn_heads.reshape(heads_kv, group_size, tok_rows, HD)
        .transpose(2, 0, 1, 3)
        .reshape(tok_rows, heads_query * HD)
        .astype(jnp.bfloat16)
    )
    mixed = residual.astype(jnp.float32) + attn.astype(jnp.float32)
    local_squares = jnp.sum(mixed * mixed, axis=1)
    total_squares = lax.psum(local_squares, "exp")
    normed = (mixed * lax.rsqrt(total_squares / D + 1e-05)[:, None] * norm_gain[None, :]).astype(
        jnp.bfloat16
    )
    feat_local = normed.shape[1]
    chosen = routes[:, 0]
    expert_ids = jnp.arange(EXPERTS, dtype=jnp.int32)
    onehot = (chosen[:, None] == expert_ids[None, :]).astype(jnp.int32)
    slot_index = jnp.sum((jnp.cumsum(onehot, axis=0) - 1) * onehot, axis=1)
    slot_ids = jnp.arange(CAP, dtype=jnp.int32)
    select = (
        (chosen[None, None, :] == expert_ids[:, None, None])
        & (slot_index[None, None, :] == slot_ids[None, :, None])
    ).astype(jnp.float32)
    packed = jnp.einsum(
        "ect,td->ecd", select.astype(jnp.bfloat16), normed, preferred_element_type=jnp.float32
    ).astype(jnp.bfloat16)
    ctx_count = lax.axis_size("ctx")
    members = ctx_count // EXPERTS
    outgoing = jnp.broadcast_to(packed[:, None], (EXPERTS, members, CAP, feat_local)).reshape(
        ctx_count, CAP, feat_local
    )
    incoming = lax.all_to_all(outgoing, "ctx", split_axis=0, concat_axis=0, tiled=True)
    slot_count = incoming.shape[1]
    flat_rows = incoming.reshape(ctx_count * slot_count, feat_local)
    gate_part = jnp.einsum("rd,fd->rf", flat_rows, w_gate, preferred_element_type=jnp.float32)
    up_part = jnp.einsum("rd,fd->rf", flat_rows, w_up, preferred_element_type=jnp.float32)
    gate_full = lax.psum(gate_part.astype(jnp.bfloat16), "exp").astype(jnp.float32)
    up_full = lax.psum(up_part.astype(jnp.bfloat16), "exp").astype(jnp.float32)
    hidden = (jax.nn.silu(gate_full) * up_full).astype(jnp.bfloat16)
    down_part = jnp.dot(hidden, w_down, preferred_element_type=jnp.float32).reshape(
        ctx_count, slot_count, feat_local
    )
    returned = lax.all_to_all(
        down_part.astype(jnp.bfloat16), "ctx", split_axis=0, concat_axis=0, tiled=True
    ).astype(down_part.dtype)
    combined = returned.reshape(EXPERTS, members, CAP, feat_local).sum(axis=1)
    moe_rows = jnp.einsum(
        "ect,ecd->td",
        select,
        combined,
        precision=lax.Precision.HIGHEST,
        preferred_element_type=jnp.float32,
    )
    return (route_weight[:, None] * moe_rows).astype(jnp.bfloat16)


def solution(mesh):
    in_specs = (
        P("ctx", "exp"),
        P("ctx", "exp"),
        P("ctx", "exp"),
        P("ctx", "exp"),
        P("exp"),
        P("ctx", None),
        P("ctx"),
        P("ctx", "exp"),
        P("ctx", "exp"),
        P("ctx", "exp"),
    )
    out_specs = P("ctx", "exp")
    return jax.shard_map(body, mesh=mesh, in_specs=in_specs, out_specs=out_specs, check_vma=False)
```

profile of v0, /device:TPU:40, one launch (start us, length us, event | category | flops | bytes accessed | tf_op | source)
XLA Modules:
  0.0 611.7 jit_solution(5762565364103222619)
XLA Ops:
  6.5 0.0 copy-start
  6.5 0.0 all-gather.3.cloned.1.call-start
  6.5 0.7 all-gather.3.cloned.1.call-update
  7.3 0.0 all-gather.5.cloned.1.call-start
  7.3 0.7 all-gather.5.cloned.1.call-update
  8.0 0.0 all-reduce.3.cloned.1.call-start
  8.1 0.7 fusion.22
  8.8 0.1 reduce_window_sum.11
  8.9 1.0 reshape.116
  9.9 0.8 select_reduce_fusion
  10.8 0.7 iota_compare_fusion.3
  11.4 128.2 %all-gather.3.cloned.1.call-done = bf16[4096,128]{1,0:T(8,128)(2,1)} async-done(((bf16[64,128]{1,0:T(8,128)(2,1)}), bf16[4096,128]{1,0:T(8,128)(2,1)}) %all-gather.3.cloned.1.call-update) | async-done | bytes 1048592 | tf_op jit(solution)/shard_map/all_gather | solution.py:32
  139.6 125.6 %all-gather.5.cloned.1.call-done = bf16[4096,128]{1,0:T(8,128)(2,1)} async-done(((bf16[64,128]{1,0:T(8,128)(2,1)}), bf16[4096,128]{1,0:T(8,128)(2,1)}) %all-gather.5.cloned.1.call-update) | async-done | bytes 1048592 | tf_op jit(solution)/shard_map/all_gather | solution.py:33
  265.2 0.0 copy-start.1
  265.2 0.0 copy-start.2
  265.2 6.3 %conditional.1 = (f32[1,384]{1,0:T(1,128)S(1)}, f32[1,384,128]{2,1,0:T(8,128)S(1)}) conditional(s32[]{:T(128)} %convert_element_type.72, () %tuple.13, (s32[]{:T(128)}, s32[6,64]{1,0:T(8,128)S(1)}, bf16[1,6,64,128]{3,1,2,0:T(8,128)(2,1)S(1)}, bf16[4096,128]{1,0:T(8,128)(2,1)}, bf16[4096,128]{1,0:T(8,128)(2,1)}) %tuple.26), branch_computations={%region_2.0_spmd, %region_3.6_spmd} | conditional | flops 824180736 | bytes 25680432 | solution.py:61
  265.2 0.1 add.30
  265.3 0.0 copy-start.6
  265.3 2.6 fusion.29
  268.0 0.0 copy-done.6
  268.0 1.9 fusion.4
  269.9 1.6 fusion.1
  271.5 0.1 divide_convert_fusion
  271.7 0.1 copy.13
  271.7 0.0 copy-done.1
  271.7 0.1 multiply_reduce_fusion
  271.9 10.3 %psum.21 = f32[64]{0:T(128)S(1)} all-reduce(f32[64]{0:T(128)S(1)} %multiply_reduce_fusion), channel_id=1, replica_groups=mesh['ctx'=64,'exp'=8] {'exp'}, use_global_device_ids=true, to_apply=%region_7.8 | all-reduce | flops 64 | bytes 512 | tf_op jit(solution)/shard_map/psum | solution.py:73
  282.2 0.0 copy-done.2
  282.2 0.2 convolution_convert_fusion.3
  282.4 0.2 broadcast_in_dim.22
  282.6 69.9 %all_to_all.10 = bf16[64,24,768]{2,1,0:T(8,128)(2,1)S(1)} all-to-all(bf16[64,24,768]{2,1,0:T(8,128)(2,1)S(1)} %bitcast.42), channel_id=1, replica_groups=mesh['ctx'=64,'exp'=8] {'ctx'}, dimensions={0} | all-to-all | bytes 4718592 | tf_op jit(solution)/shard_map/all_to_all | solution.py:95
  352.5 0.0 copy-done
  352.5 0.0 copy-start.4
  352.5 4.2 convolution_convert_fusion
  356.7 0.0 copy-done.4
  356.7 4.2 convolution_convert_fusion.1
  360.8 0.0 copy-start.5
  360.8 0.0 all-reduce.3.cloned.1.call-update
  360.9 154.0 %all-reduce.3.cloned.1.call-done = (bf16[1536,1024]{1,0:T(8,128)(2,1)}, bf16[1536,1024]{1,0:T(8,128)(2,1)}) async-done(((bf16[1536,1024]{1,0:T(8,128)(2,1)}, bf16[1536,1024]{1,0:T(8,128)(2,1)}), (bf16[1536,1024]{1,0:T(8,128)(2,1)}, bf16[1536,1024]{1,0:T(8,128)(2,1)})) %all-reduce.3.cloned.1.call-update) | async-done | bytes 6291472 | tf_op jit(solution)/shard_map/psum | solution.py:101
  514.9 0.0 copy-done.5
  514.9 6.7 %convolution_convert_fusion.2 = bf16[1536,768]{1,0:T(8,128)(2,1)S(1)} fusion(bf16[1024,768]{1,0:T(8,128)(2,1)S(1)} %copy-done.5, bf16[1536,1024]{1,0:T(8,128)(2,1)} %get-tuple-element.33, bf16[1536,1024]{1,0:T(8,128)(2,1)} %get-tuple-element.34), kind=kOutput, calls=%fused_computation.20 | convolution fusion | flops 2429681664 | bytes 10223616 | tf_op jit(solution)/shard_map/dot_general | solution.py:103
  521.6 0.0 copy-start.3
  521.6 82.3 %all_to_all.11 = bf16[64,24,768]{2,1,0:T(8,128)(2,1)S(1)} all-to-all(bf16[64,24,768]{2,1,0:T(8,128)(2,1)S(1)} %bitcast.45), channel_id=1, replica_groups=mesh['ctx'=64,'exp'=8] {'ctx'}, dimensions={0} | all-to-all | bytes 4718592 | tf_op jit(solution)/shard_map/all_to_all | solution.py:106
  603.9 0.3 convert_reduce_fusion
  604.2 0.0 copy-done.3
  604.2 0.9 fusion.15
  (8 shorter events, 0.1 us)
Async XLA Ops:
  6.5 345.9 %copy-start = (bf16[1024,768]{1,0:T(8,128)(2,1)S(1)}, bf16[1024,768]{1,0:T(8,128)(2,1)}, u32[]{:S(2)}) copy-start(bf16[1024,768]{1,0:T(8,128)(2,1)} %param.20) | copy-start | bytes 4718596
  6.5 133.1 %all-gather.3.cloned.1.call-start = ((), (), s32[]{:S(2)}) async-start(), calls=%async_computation.2 | async-start | bytes 1064960 | tf_op jit(solution)/shard_map/all_gather | solution.py:32
  7.3 257.9 %all-gather.5.cloned.1.call-start = ((), (), s32[]{:S(2)}) async-start(), calls=%async_computation.3 | async-start | bytes 1064960 | tf_op jit(solution)/shard_map/all_gather | solution.py:33
  8.0 506.9 %all-reduce.3.cloned.1.call-start = ((), (), s32[]{:S(2)}) async-start(), calls=%async_computation.4 | async-start | bytes 12582912 | tf_op jit(solution)/shard_map/psum | solution.py:101
  265.2 6.5 %copy-start.1 = (bf16[64,768]{1,0:T(8,128)(2,1)S(1)}, bf16[64,768]{1,0:T(8,128)(2,1)}, u32[]{:S(2)}) copy-start(bf16[64,768]{1,0:T(8,128)(2,1)} %param.15) | copy-start | bytes 294916
  265.2 17.0 %copy-start.2 = (f32[768]{0:T(1024)S(1)}, f32[768]{0:T(1024)}, u32[]{:S(2)}) copy-start(f32[768]{0:T(1024)} %param.16) | copy-start | bytes 9220
  265.3 2.7 copy-start.6
  352.5 4.2 copy-start.4
  360.8 154.0 %copy-start.5 = (bf16[1024,768]{1,0:T(8,128)(2,1)S(1)}, bf16[1024,768]{1,0:T(8,128)(2,1)}, u32[]{:S(2)}) copy-start(bf16[1024,768]{1,0:T(8,128)(2,1)} %param.21) | copy-start | bytes 4718596
  521.6 82.6 %copy-start.3 = (f32[64]{0:T(128)S(1)}, f32[64]{0:T(128)}, u32[]{:S(2)}) copy-start(f32[64]{0:T(128)} %param.18) | copy-start | bytes 772
Sparse Core Ops, SparseCore 0:
  11.7 127.8 all-gather.2
  144.0 121.1 all-gather.4
  361.0 153.8 all-reduce.2
where the time goes:
time: 612 us
  waiting for transfers between devices  409 us (67%)
  blocking collectives  162 us (26%)
  matrix products  20.8 us (3%)
  between operations  13.2 us (2%)
    psum x1, waiting for transfers between devices, body(): up_full = lax.psum(up_part.astype(jnp.bfloat16), 'exp').astype(jnp.float32)  154 us
    all_gather x1, waiting for transfers between devices, body(): key_shard = lax.all_gather(keys, 'ctx', axis=0, tiled=True)  128 us
    all_gather x1, waiting for transfers between devices, body(): value_shard = lax.all_gather(values, 'ctx', axis=0, tiled=True)  126 us
    all_to_all x1, blocking collectives, body(): lax.all_to_all(down_part.astype(jnp.bfloat16), 'ctx', split_axis=0, conca...  82.3 us
    all_to_all x1, blocking collectives, body(): lax.all_to_all(outgoing, 'ctx', split_axis=0, concat_axis=0, tiled=True)  69.9 us
  transfers between devices with their start and end apart: 3, of which 3 were waited for; matrix products, arithmetic and copies ran while one was open for 1% of the time, Pallas kernels for 0%

commit v1 on v0

--- a/solution.py
+++ b/solution.py
@@ -8,6 +8,12 @@
 HD = 128
 EXPERTS = 4
 CAP = 24
+
+
+def add_all(value, axis):
+    pieces = lax.all_gather(value, axis, axis=0, tiled=False)
+    summed = pieces.sum(axis=0)
+    return summed
 
 
 def body(queries, keys, values, residual, norm_gain, routes, route_weight, w_gate, w_up, w_down):
@@ -98,7 +104,7 @@
     gate_part = jnp.einsum("rd,fd->rf", flat_rows, w_gate, preferred_element_type=jnp.float32)
     up_part = jnp.einsum("rd,fd->rf", flat_rows, w_up, preferred_element_type=jnp.float32)
     gate_full = lax.psum(gate_part.astype(jnp.bfloat16), "exp").astype(jnp.float32)
-    up_full = lax.psum(up_part.astype(jnp.bfloat16), "exp").astype(jnp.float32)
+    up_full = add_all(up_part.astype(jnp.bfloat16), "exp").astype(jnp.float32)
     hidden = (jax.nn.silu(gate_full) * up_full).astype(jnp.bfloat16)
     down_part = jnp.dot(hidden, w_down, preferred_element_type=jnp.float32).reshape(
         ctx_count, slot_count, feat_local

time: 612 us -> 802 us (1.31)
  the two profiles are of different devices: /device:TPU:40 before, /device:TPU:8 now
where the time goes in v1:
time: 802 us
  waiting for transfers between devices  582 us (73%)
  blocking collectives  160 us (20%)
  matrix products  22.3 us (3%)
  other arithmetic  20.2 us (3%)
  between operations  13.2 us (2%)
    all_gather x1, waiting for transfers between devices, add_all(): pieces = lax.all_gather(value, axis, axis=0, tiled=False)  240 us
    all_gather x1, waiting for transfers between devices, body(): key_shard = lax.all_gather(keys, 'ctx', axis=0, tiled=True)  132 us
    all_gather x1, waiting for transfers between devices, body(): value_shard = lax.all_gather(values, 'ctx', axis=0, tiled=True)  126 us
    psum x1, waiting for transfers between devices, body(): lax.psum(gate_part.astype(jnp.bfloat16), 'exp').astype(jnp.float32)  83 us
    all_to_all x1, blocking collectives, body(): lax.all_to_all(down_part.astype(jnp.bfloat16), 'ctx', split_axis=0, conca...  79.2 us
    all_to_all x1, blocking collectives, body(): lax.all_to_all(outgoing, 'ctx', split_axis=0, concat_axis=0, tiled=True)  70 us
  transfers between devices with their start and end apart: 4, of which 4 were waited for; matrix products, arithmetic and copies ran while one was open for 3% of the time, Pallas kernels for 0%

profile of v1, /device:TPU:8, one launch (start us, length us, event | category | flops | bytes accessed | tf_op | source)
XLA Modules:
  0.0 801.9 jit_solution(9677162956938436703)
XLA Ops:
  6.5 0.0 copy-start
  6.5 0.0 all-gather.5.cloned.1.call-start
  6.5 0.7 all-gather.5.cloned.1.call-update
  7.3 0.0 all-gather.7.cloned.1.call-start
  7.3 0.7 all-gather.7.cloned.1.call-update
  8.0 0.0 all-gather.9.cloned.1.call-start
  8.1 0.7 fusion.22
  8.8 0.1 reduce_window_sum.11
  8.9 1.0 reshape.116
  9.9 0.8 select_reduce_fusion
  10.8 0.7 iota_compare_fusion.3
  11.4 131.6 %all-gather.5.cloned.1.call-done = bf16[4096,128]{1,0:T(8,128)(2,1)} async-done(((bf16[64,128]{1,0:T(8,128)(2,1)}), bf16[4096,128]{1,0:T(8,128)(2,1)}) %all-gather.5.cloned.1.call-update) | async-done | bytes 1048592 | tf_op jit(solution)/shard_map/all_gather | solution.py:38
  143.0 125.6 %all-gather.7.cloned.1.call-done = bf16[4096,128]{1,0:T(8,128)(2,1)} async-done(((bf16[64,128]{1,0:T(8,128)(2,1)}), bf16[4096,128]{1,0:T(8,128)(2,1)}) %all-gather.7.cloned.1.call-update) | async-done | bytes 1048592 | tf_op jit(solution)/shard_map/all_gather | solution.py:39
  268.6 0.0 copy-start.2
  268.6 6.3 conditional.1
  268.6 0.1 add.28
  268.7 0.0 copy-start.7
  268.7 2.6 fusion.29
  271.3 0.0 copy-done.7
  271.4 1.9 fusion.4
  273.3 1.6 fusion.1
  274.9 0.1 divide_convert_fusion
  275.0 0.1 copy.13
  275.1 0.0 copy-done.2
  275.1 0.1 multiply_reduce_fusion
  275.2 10.8 %psum.14 = f32[64]{0:T(128)S(1)} all-reduce(f32[64]{0:T(128)S(1)} %multiply_reduce_fusion), channel_id=1, replica_groups=mesh['ctx'=64,'exp'=8] {'exp'}, use_global_device_ids=true, to_apply=%region_7.8 | all-reduce | flops 64 | bytes 512 | tf_op jit(solution)/shard_map/psum | solution.py:79
  286.1 0.0 copy-done.3
  286.1 0.2 convolution_convert_fusion.3
  286.3 0.2 broadcast_in_dim.22
  286.5 70.0 %all_to_all.10 = bf16[64,24,768]{2,1,0:T(8,128)(2,1)S(1)} all-to-all(bf16[64,24,768]{2,1,0:T(8,128)(2,1)S(1)} %bitcast.44), channel_id=1, replica_groups=mesh['ctx'=64,'exp'=8] {'ctx'}, dimensions={0} | all-to-all | bytes 4718592 | tf_op jit(solution)/shard_map/all_to_all | solution.py:101
  356.4 1.5 copy-done.1
  358.0 0.0 copy-done
  358.0 4.1 convolution_convert_fusion
  362.1 0.0 all-gather.9.cloned.1.call-update
  362.1 0.2 all-reduce.2.cloned.1.call-start
  362.3 1.2 copy-done.5
  363.5 5.7 convolution_convert_fusion.1
  369.2 0.0 all-reduce.2.cloned.1.call-update
  369.2 240.2 %all-gather.9.cloned.1.call-done = bf16[12288,1024]{1,0:T(8,128)(2,1)} async-done(((bf16[1536,1024]{1,0:T(8,128)(2,1)}), bf16[12288,1024]{1,0:T(8,128)(2,1)}) %all-gather.9.cloned.1.call-update) | async-done | bytes 25165840 | tf_op jit(solution)/shard_map/all_gather | solution.py:14
  609.5 15.7 %reduce_sum.52 = bf16[1536,1024]{1,0:T(8,128)(2,1)} reduce(bf16[8,1536,1024]{2,1,0:T(8,128)(2,1)} %bitcast.43, bf16[]{:T(256)} %constant.44.clone.1), dimensions={0}, to_apply=%region_9.10 | reduce | flops 11010048 | bytes 28311554 | tf_op jit(solution)/shard_map/reduce_sum | solution.py:15
  625.1 83.0 %all-reduce.2.cloned.1.call-done = bf16[1536,1024]{1,0:T(8,128)(2,1)} async-done(((bf16[1536,1024]{1,0:T(8,128)(2,1)}), bf16[1536,1024]{1,0:T(8,128)(2,1)}) %all-reduce.2.cloned.1.call-update) | async-done | bytes 3145744 | tf_op jit(solution)/shard_map/psum | solution.py:106
  708.1 0.0 copy-done.6
  708.1 6.7 convolution_convert_fusion.2
  714.8 0.0 copy-start.4
  714.9 79.2 %all_to_all.11 = bf16[64,24,768]{2,1,0:T(8,128)(2,1)S(1)} all-to-all(bf16[64,24,768]{2,1,0:T(8,128)(2,1)S(1)} %bitcast.47), channel_id=1, replica_groups=mesh['ctx'=64,'exp'=8] {'ctx'}, dimensions={0} | all-to-all | bytes 4718592 | tf_op jit(solution)/shard_map/all_to_all | solution.py:112
  794.1 0.3 convert_reduce_fusion
  794.4 0.0 copy-done.4
  794.4 0.9 fusion.15
  (12 shorter events, 0.1 us)
Async XLA Ops:
  6.5 351.4 %copy-start = (bf16[1024,768]{1,0:T(8,128)(2,1)S(1)}, bf16[1024,768]{1,0:T(8,128)(2,1)}, u32[]{:S(2)}) copy-start(bf16[1024,768]{1,0:T(8,128)(2,1)} %param.20) | copy-start | bytes 4718596
  6.5 136.5 %all-gather.5.cloned.1.call-start = ((), (), s32[]{:S(2)}) async-start(), calls=%async_computation.2 | async-start | bytes 1064960 | tf_op jit(solution)/shard_map/all_gather | solution.py:38
  7.3 261.3 %all-gather.7.cloned.1.call-start = ((), (), s32[]{:S(2)}) async-start(), calls=%async_computation.3 | async-start | bytes 1064960 | tf_op jit(solution)/shard_map/all_gather | solution.py:39
  8.0 601.5 %all-gather.9.cloned.1.call-start = ((), (), s32[]{:S(2)}) async-start(), calls=%async_computation.5 | async-start | bytes 28311552 | tf_op jit(solution)/shard_map/all_gather | solution.py:14
  268.6 6.5 copy-start.2
  268.6 17.5 %copy-start.3 = (f32[768]{0:T(1024)S(1)}, f32[768]{0:T(1024)}, u32[]{:S(2)}) copy-start(f32[768]{0:T(1024)} %param.16) | copy-start | bytes 9220
  268.7 2.7 copy-start.7
  356.4 1.5 copy-start.1
  362.1 1.4 copy-start.5
  362.1 346.0 %all-reduce.2.cloned.1.call-start = ((), (), s32[]{:S(2)}) async-start(), calls=%async_computation.4 | async-start | bytes 6291456 | tf_op jit(solution)/shard_map/psum | solution.py:106
  609.5 98.7 %copy-start.6 = (bf16[1024,768]{1,0:T(8,128)(2,1)S(1)}, bf16[1024,768]{1,0:T(8,128)(2,1)}, u32[]{:S(2)}) copy-start(bf16[1024,768]{1,0:T(8,128)(2,1)} %param.21) | copy-start | bytes 4718596
  714.8 79.5 %copy-start.4 = (f32[64]{0:T(128)S(1)}, f32[64]{0:T(128)}, u32[]{:S(2)}) copy-start(f32[64]{0:T(128)} %param.18) | copy-start | bytes 772
Sparse Core Ops, SparseCore 0:
  11.7 131.2 all-gather.4
  147.4 121.1 all-gather.6
  362.2 247.2 all-gather.8
  612.3 95.8 all-reduce.1
